TPU v7x, 32 devices: a whole 2x2x4 slice. The times are simulated.
32 devices in a mesh: groups: 2 (over y), passage: 8 (over z, x), tensor: 2 (over core).
Axes of the slice: x: 2, y: 2, z: 4, core: 2. Of those that a mesh axis runs over, the one named last changes fastest.
Arguments:
- corpus: bfloat16 [96, 256, 1024], P(('groups', 'passage')), parts along dimension 0, may hold values from -6 to 6
- queries: bfloat16 [32, 2048], P(('groups', 'passage'), 'tensor'), parts along dimension 0, may hold values from -180 to 180
- key_weight: bfloat16 [1024, 2048], P('passage', 'tensor'), may hold values from -0.1875 to 0.1875
- value_weight: bfloat16 [1024, 2048], P('passage', 'tensor'), may hold values from -0.1875 to 0.1875
- retrieved: int32 [2, 16], P('groups'), parts along dimension 0, may hold values from 0 to 47, as said below
- placement_map: int32 [96], P('groups'), parts along dimension 0, may hold values from 0 to 47, as said below
- valid_counts: int32 [96], P('groups'), parts along dimension 0, may hold values from 16 to 256
Outputs:
- context: bfloat16 [32, 2048], P(('groups', 'passage'), 'tensor'), parts along dimension 0
There are 2 independent parts, one for each index of `groups`. A program takes and returns all parts, laid end to end along the dimension named above; an argument that names none is the same for every part. Nothing has to cross between parts.
Inputs may be any that keep to these rules, and one draw needn't show every extreme that they name: Each row lists 16 ids; all 16 retrieved ids are distinct. With shard = placement_map[id] // 6, at most 5 retrieved passages lie on one shard, and some shard holds exactly 5. `placement_map`: A permutation of the corpus rows.
All inputs are finite; a program needn't handle non-finite values.
Results may differ from a plain program's by a relative error of at most 0.01.
The roundings to bfloat16 on the way count: a program that leaves them out, or rounds other values in their place, can miss the bound.
Values may be sent and summed in bfloat16 or wider, within the bound.
A program may use at most 64 MiB of HBM per device.

v0:
```python
import jax
import jax.numpy as jnp
from jax import lax
from jax.sharding import PartitionSpec as P

DH = 64
LEN = 256
MOST = 5
QT = 16


def normalize(hidden):
    values32 = hidden.astype(jnp.float32)
    factor = lax.rsqrt(jnp.mean(values32 * values32, axis=-1, keepdims=True) + 1e-06)
    return (values32 * factor).astype(jnp.bfloat16)


def widen(stats):
    return jnp.repeat(stats, DH, axis=-1)


def join_partials(first, second):
    top_one, mass_one, ctx_one = first
    top_two, mass_two, ctx_two = second
    highest = jnp.maximum(top_one, top_two)
    scale_one = jnp.exp(top_one - highest)
    scale_two = jnp.exp(top_two - highest)
    return (
        highest,
        mass_one * scale_one + mass_two * scale_two,
        ctx_one * widen(scale_one) + ctx_two * widen(scale_two),
    )


def on_device(corpus, queries, key_weight, value_weight, retrieved, placement_map, valid_counts):
    shard_index = lax.axis_index("passage")
    corp_rows = corpus.shape[0]
    per_question = retrieved.shape[1]
    total_ret = retrieved.shape[0] * per_question
    flat_ids = retrieved.reshape(total_ret)
    corpus_row = placement_map[flat_ids]
    lengths = valid_counts[flat_ids]
    owned_mask = corpus_row // corp_rows == shard_index
    owner_rank = jnp.cumsum(owned_mask.astype(jnp.int32)) - 1
    slot_iota = jnp.arange(MOST, dtype=jnp.int32)
    selector = (owned_mask[None, :] & (owner_rank[None, :] == slot_iota[:, None])).astype(jnp.int32)
    local_rows = jnp.sum(selector * (corpus_row % corp_rows)[None, :], axis=1)
    slot_lengths = jnp.sum(selector * lengths[None, :], axis=1)
    question_ids = jnp.arange(total_ret, dtype=jnp.int32) // per_question
    slot_question = jnp.sum(selector * question_ids[None, :], axis=1)
    passages = corpus[local_rows]
    normed = normalize(passages).reshape(MOST * LEN, passages.shape[2])
    full_key, full_value = (
        lax.all_gather(key_weight, "passage", axis=0, tiled=True),
        lax.all_gather(value_weight, "passage", axis=0, tiled=True),
    )
    width = key_weight.shape[1]
    heads = width // DH
    key_rows = jnp.dot(normed, full_key, preferred_element_type=jnp.float32).astype(jnp.bfloat16)
    value_rows = jnp.dot(normed, full_value, preferred_element_type=jnp.float32).astype(
        jnp.bfloat16
    )
    key_rows = key_rows.reshape(MOST, LEN, heads, DH)
    value_rows = value_rows.reshape(MOST, LEN, heads, DH)
    all_queries = lax.all_gather(queries, "passage", axis=0, tiled=True)
    query_total = all_queries.shape[0]
    best_score = jnp.full((query_total, heads), -1e30, jnp.float32)
    row_total = jnp.zeros((query_total, heads), jnp.float32)
    context_sum = jnp.zeros((query_total, width), jnp.float32)
    positions = jnp.arange(LEN, dtype=jnp.int32)
    scaling = DH ** (-0.5)
    for number in range(MOST):
        first_row = slot_question[number] * QT
        block = lax.dynamic_slice_in_dim(all_queries, first_row, QT, 0).reshape(QT, heads, DH)
        scores = (
            jnp.einsum("thd,lhd->htl", block, key_rows[number], preferred_element_type=jnp.float32)
            * scaling
        )
        live_mask = (positions < slot_lengths[number])[None, None, :]
        scores = jnp.where(live_mask, scores, jnp.float32(-1e30))
        top_score = jnp.max(scores, axis=-1)
        weights = jnp.where(live_mask, jnp.exp(scores - top_score[..., None]), jnp.float32(0.0))
        row_mass = jnp.sum(weights, axis=-1)
        partial_ctx = jnp.einsum(
            "htl,lhd->thd",
            weights.astype(jnp.bfloat16),
            value_rows[number],
            preferred_element_type=jnp.float32,
        ).reshape(QT, width)
        old_state = (
            lax.dynamic_slice_in_dim(best_score, first_row, QT, 0),
            lax.dynamic_slice_in_dim(row_total, first_row, QT, 0),
            lax.dynamic_slice_in_dim(context_sum, first_row, QT, 0),
        )
        new_top, new_mass, new_ctx = join_partials(
            old_state, (top_score.T, row_mass.T, partial_ctx)
        )
        best_score = lax.dynamic_update_slice_in_dim(best_score, new_top, first_row, 0)
        row_total = lax.dynamic_update_slice_in_dim(row_total, new_mass, first_row, 0)
        context_sum = lax.dynamic_update_slice_in_dim(context_sum, new_ctx, first_row, 0)
    global_top = lax.pmax(best_score, "passage")
    rescale = jnp.exp(best_score - global_top)
    own_mass, own_ctx = (
        lax.psum_scatter(row_total * rescale, "passage", scatter_dimension=0, tiled=True),
        lax.psum_scatter(context_sum * widen(rescale), "passage", scatter_dimension=0, tiled=True),
    )
    return (own_ctx / widen(own_mass)).astype(jnp.bfloat16)


def solution(mesh):
    in_specs = (
        P(("groups", "passage"), None, None),
        P(("groups", "passage"), "tensor"),
        P("passage", "tensor"),
        P("passage", "tensor"),
        P("groups", None),
        P("groups"),
        P("groups"),
    )
    out_specs = P(("groups", "passage"), "tensor")
    return jax.shard_map(
        on_device, mesh=mesh, in_specs=in_specs, out_specs=out_specs, check_vma=False
    )
```

profile of v0, /device:TPU:0, one launch (start us, length us, event | category | flops | bytes accessed | tf_op | source)
XLA Modules:
  0.0 196.4 jit_solution(11612404778578878747)
XLA Ops:
  6.5 0.7 all-gather.4.cloned.1.call-update
  7.3 0.7 all-gather.6.cloned.1.call-update
  8.1 0.7 fusion.84
  8.7 1.3 gather_fusion
  10.4 1.3 gather_fusion.1
  11.9 2.4 %gather_fusion.2 = bf16[5,256,1024]{2,1,0:T(8,128)(2,1)} fusion(bf16[6,256,1024]{2,1,0:T(8,128)(2,1)S(1)} %copy-done, s32[1024]{0:T(1024)S(1)} %pad_clamp_fusion), kind=kCustom, calls=%fused_computation.2 | custom fusion | bytes 5242900 | tf_op jit(solution)/shard_map/gather | solution.py:51
  14.3 2.3 %multiply_reduce_fusion = f32[5,256]{1,0:T(8,128)S(1)} fusion(bf16[5,256,1024]{2,1,0:T(8,128)(2,1)} %gather_fusion.2), kind=kLoop, calls=%fused_computation.5 | loop fusion | flops 3930880 | bytes 2626560 | tf_op jit(solution)/shard_map/reduce_sum | solution.py:14
  16.7 0.7 fusion.99
  17.3 0.7 iota_compare_fusion.4
  18.0 32.4 %all-gather = bf16[8,2,1024]{2,1,0:T(2,128)(2,1)S(1)} all-gather(bf16[1,2,1024]{2,1,0:T(2,128)(2,1)S(1)} %bitcast.194), channel_id=1, replica_groups=mesh['groups'=2,'passage'=8,'tensor'=2] {'passage'}, dimensions={0}, use_global_device_ids=true | all-gather | bytes 36864 | tf_op jit(solution)/shard_map/all_gather | solution.py:65
  50.6 0.6 dynamic-slice
  51.9 0.7 iota_compare_fusion.5
  52.5 0.6 iota_compare_fusion.2
  53.2 0.6 iota_compare_fusion.3
  53.8 0.6 iota_compare_fusion.1
  54.4 3.8 %fusion = bf16[1280,1024]{1,0:T(8,128)(2,1)} fusion(f32[1280]{0:T(1024)S(1)} %rsqrt.12, bf16[5,256,1024]{2,1,0:T(8,128)(2,1)} %gather_fusion.2), kind=kLoop, calls=%fused_computation.4 | loop fusion | flops 3932160 | bytes 5248000 | tf_op jit(solution)/shard_map/convert_element_type | solution.py:15
  58.2 3.6 %all-gather.4.cloned.1.call-done = bf16[1024,1024]{1,0:T(8,128)(2,1)} async-done(((bf16[128,1024]{1,0:T(8,128)(2,1)}), bf16[1024,1024]{1,0:T(8,128)(2,1)}) %all-gather.4.cloned.1.call-update) | async-done | bytes 2097168 | tf_op jit(solution)/shard_map/all_gather | solution.py:54
  61.8 5.3 %convolution_convert_fusion.1 = bf16[1280,1024]{0,1:T(8,128)(2,1)S(1)} fusion(bf16[1280,1024]{1,0:T(8,128)(2,1)} %fusion, bf16[1024,1024]{1,0:T(8,128)(2,1)} %all-gather.4.cloned.1.call-done), kind=kOutput, calls=%fused_computation.7 | convolution fusion | flops 2685665280 | bytes 7340032 | tf_op jit(solution)/shard_map/dot_general | solution.py:59
  67.3 0.9 fusion.104
  68.2 0.9 fusion.100
  69.4 0.9 fusion.103
  70.3 0.9 fusion.101
  71.2 19.5 %pmax.7 = f32[16,16]{0,1:T(8,128)S(1)} all-reduce(f32[16,16]{0,1:T(8,128)S(1)} %get-tuple-element.17), channel_id=1, replica_groups=mesh['groups'=2,'passage'=8,'tensor'=2] {'passage'}, use_global_device_ids=true, to_apply=%region_9.10 | all-reduce | flops 256 | bytes 2048 | tf_op jit(solution)/shard_map/pmax | solution.py:101
  90.7 1.1 fusion.34
  91.8 20.2 %all-gather.6.cloned.1.call-done = bf16[1024,1024]{1,0:T(8,128)(2,1)} async-done(((bf16[128,1024]{1,0:T(8,128)(2,1)}), bf16[1024,1024]{1,0:T(8,128)(2,1)}) %all-gather.6.cloned.1.call-update) | async-done | bytes 2097168 | tf_op jit(solution)/shard_map/all_gather | solution.py:55
  112.0 5.3 %convolution_convert_fusion = bf16[1280,1024]{0,1:T(8,128)(2,1)S(1)} fusion(bf16[1280,1024]{1,0:T(8,128)(2,1)} %fusion, bf16[1024,1024]{1,0:T(8,128)(2,1)} %all-gather.6.cloned.1.call-done), kind=kOutput, calls=%fused_computation.6 | convolution fusion | flops 2685665280 | bytes 7340032 | tf_op jit(solution)/shard_map/dot_general | solution.py:60
  117.6 0.7 copy-done.2
  119.9 0.3 fusion.16
  120.7 0.7 reshape.298
  121.4 19.2 %all-reduce.1 = f32[16,16]{0,1:T(8,128)S(1)} all-reduce(f32[16,16]{0,1:T(8,128)S(1)} %get-tuple-element.34), channel_id=3, replica_groups=mesh['groups'=2,'passage'=8,'tensor'=2] {'passage'}, use_global_device_ids=true, to_apply=%region_16.17.clone | all-reduce | flops 256 | bytes 2048
  141.0 47.6 %all-reduce.4.cloned.1.call-done = f32[16,1024]{1,0:T(8,128)} async-done(((f32[16,1024]{1,0:T(8,128)}), f32[16,1024]{1,0:T(8,128)}) %all-reduce.4.cloned.1.call-update) | async-done | bytes 65552
  188.6 1.4 fusion.81
  (51 shorter events, 3.7 us)
Async XLA Ops:
  6.5 5.4 %copy-start = (bf16[6,256,1024]{2,1,0:T(8,128)(2,1)S(1)}, bf16[6,256,1024]{2,1,0:T(8,128)(2,1)}, u32[]{:S(2)}) copy-start(bf16[6,256,1024]{2,1,0:T(8,128)(2,1)} %param.7) | copy-start | bytes 9437188
  6.5 55.3 %all-gather.4.cloned.1.call-start = ((), (), s32[]{:S(2)}) async-start(), calls=%async_computation | async-start | bytes 2359296 | tf_op jit(solution)/shard_map/all_gather | solution.py:54
  7.3 104.8 %all-gather.6.cloned.1.call-start = ((), (), s32[]{:S(2)}) async-start(), calls=%async_computation.1 | async-start | bytes 2359296 | tf_op jit(solution)/shard_map/all_gather | solution.py:55
  8.0 180.6 %all-reduce.4.cloned.1.call-start = ((), (), s32[]{:S(2)}) async-start(), calls=%async_computation.2 | async-start | bytes 131072
  14.3 3.7 %copy-start.7 = (bf16[2,1024]{1,0:T(2,128)(2,1)S(1)}, bf16[2,1024]{1,0:T(2,128)(2,1)}, u32[]{:S(2)}) copy-start(bf16[2,1024]{1,0:T(2,128)(2,1)} %param.8) | copy-start | bytes 12292
  14.3 36.3 %copy-start.8 = (u32[32]{0:T(128)S(1)}, u32[32]{0:T(128)}, u32[]{:S(2)}) copy-start(u32[32]{0:T(128)} %constant.68) | copy-start | bytes 388
  54.4 36.3 %copy-start.5 = (pred[256]{0:T(512)(128)(4,1)}, pred[256]{0:T(512)(128)(4,1)S(1)}, u32[]{:S(2)}) copy-start(pred[256]{0:T(512)(128)(4,1)S(1)} %iota_compare_fusion.1) | copy-start | bytes 772
  117.4 1.0 copy-start.2
  117.4 1.0 copy-start.4
  117.4 1.3 copy-start.3
  118.7 1.6 copy-start.1
  118.7 1.6 copy-start.6
Sparse Core Ops, SparseCore 0:
  9.5 52.2 all-gather.3
  63.9 48.0 all-gather.5
  121.5 66.9 all-reduce.3
where the time goes:
time: 197 us; the launch traced here: 196 us
  waiting for transfers between devices  72.9 us (37%)
  blocking collectives  71.1 us (36%)
  matrix products  16.1 us (8%)
  between operations  14.1 us (7%)
  other arithmetic  13.3 us (7%)
  local copies, waits for them, and re-layouts  8.89 us (5%)
    unnamed x4, waiting for transfers between devices  49 us
    all_gather x1, blocking collectives, on_device(): all_queries = lax.all_gather(queries, 'passage', axis=0, tiled=True)  32.4 us
    all_gather x1, waiting for transfers between devices, on_device(): lax.all_gather(value_weight, 'passage', axis=0, tiled=True)  20.2 us
    pmax x1, blocking collectives, on_device(): global_top = lax.pmax(best_score, 'passage')  19.5 us
    unnamed x1, blocking collectives  19.2 us
    dot_general x1, matrix products, on_device(): jnp.dot(normed, full_key, preferred_element_type=jnp.float32)  5.32 us
    dot_general x1, matrix products, on_device(): jnp.dot(normed, full_value, preferred_element_type=jnp.float32)  5.31 us
  transfers between devices with their start and end apart: 3, of which 3 were waited for; matrix products, arithmetic and copies ran while one was open for 14% of the time, Pallas kernels for 0%

commit v1 on v0

--- a/solution.py
+++ b/solution.py
@@ -7,6 +7,18 @@
 LEN = 256
 MOST = 5
 QT = 16
+
+
+def gather_by_bits(shard, axis, dim):
+    ways, here = (lax.axis_size(axis), lax.axis_index(axis))
+    grown, reach = (shard, 1)
+    while reach < ways:
+        theirs = lax.ppermute(grown, axis, [(d, d ^ reach) for d in range(ways)])
+        mine_first = jnp.concatenate([grown, theirs], axis=dim)
+        theirs_first = jnp.concatenate([theirs, grown], axis=dim)
+        grown = jnp.where(here & reach == 0, mine_first, theirs_first)
+        reach = 2 * reach
+    return grown
 
 
 def normalize(hidden):
@@ -52,7 +64,7 @@
     normed = normalize(passages).reshape(MOST * LEN, passages.shape[2])
     full_key, full_value = (
         lax.all_gather(key_weight, "passage", axis=0, tiled=True),
-        lax.all_gather(value_weight, "passage", axis=0, tiled=True),
+        gather_by_bits(value_weight, "passage", 0),
     )
     width = key_weight.shape[1]
     heads = width // DH

time: 197 us -> 254 us (1.29)
  blocking collectives: 71.1 us -> 119 us
  waiting for transfers between devices: 72.9 us -> 65.1 us
  starting transfers between devices: 0.08 us -> 7.39 us
  other arithmetic: 13.3 us -> 18 us
  matrix products: 16.1 us -> 19.2 us
    all_gather x1, blocking collectives: 32.4 us -> 82.5 us  [on_device(): all_queries = lax.all_gather(queries, 'passage', axis=0, tiled=True)]
    all_gather x1 -> x0, waiting for transfers between devices: 20.2 us -> none  [on_device(): lax.all_gather(value_weight, 'passage', axis=0, tiled=True)]
    ppermute x0 -> x3, waiting for transfers between devices: none -> 16.7 us  [gather_by_bits(): theirs = lax.ppermute(grown, axis, [(d, d ^ reach) for d in range(ways)])]
    ppermute x0 -> x3, starting transfers between devices: none -> 7.34 us  [gather_by_bits(): theirs = lax.ppermute(grown, axis, [(d, d ^ reach) for d in range(ways)])]
    select_n x0 -> x2, other arithmetic: none -> 5.01 us  [gather_by_bits(): grown = jnp.where(here & reach == 0, mine_first, theirs_first)]
    all_gather x1, waiting for transfers between devices: 3.64 us -> 0.01 us  [on_device(): lax.all_gather(key_weight, 'passage', axis=0, tiled=True)]
    dot_general x5, matrix products: 1.59 us -> 4.41 us  [on_device(): jnp.einsum('htl,lhd->thd', weights.astype(jnp.bfloat16), value_rows[numbe...]
    unnamed x4 -> x3, waiting for transfers between devices: 49 us -> 48.4 us
  transfers between devices with their start and end apart: 3 -> 5, of which waited for: 3 -> 3; matrix products, arithmetic and copies ran while one was open for 14% -> 11% of each run, Pallas kernels for 0% -> 0%
where the time goes in v1:
time: 254 us
  blocking collectives  119 us (47%)
  waiting for transfers between devices  65.1 us (26%)
  matrix products  19.2 us (8%)
  other arithmetic  18 us (7%)
  between operations  14.5 us (6%)
  local copies, waits for them, and re-layouts  10.1 us (4%)
  starting transfers between devices  7.39 us (3%)
    all_gather x1, blocking collectives, on_device(): all_queries = lax.all_gather(queries, 'passage', axis=0, tiled=True)  82.5 us
    unnamed x3, waiting for transfers between devices  48.4 us
    unnamed x1, blocking collectives  19.1 us
    pmax x1, blocking collectives, on_device(): global_top = lax.pmax(best_score, 'passage')  17.8 us
    ppermute x3, waiting for transfers between devices, gather_by_bits(): theirs = lax.ppermute(grown, axis, [(d, d ^ reach) for d in range(ways)])  16.7 us
    ppermute x3, starting transfers between devices, gather_by_bits(): theirs = lax.ppermute(grown, axis, [(d, d ^ reach) for d in range(ways)])  7.34 us
    dot_general x1, matrix products, on_device(): jnp.dot(normed, full_value, preferred_element_type=jnp.float32)  6.25 us
    dot_general x1, matrix products, on_device(): jnp.dot(normed, full_key, preferred_element_type=jnp.float32)  5.31 us
  transfers between devices with their start and end apart: 5, of which 3 were waited for; matrix products, arithmetic and copies ran while one was open for 11% of the time, Pallas kernels for 0%

profile of v1, /device:TPU:0, one launch (start us, length us, event | category | flops | bytes accessed | tf_op | source)
XLA Modules:
  0.0 253.7 jit_solution(4850664516846533297)
XLA Ops:
  6.5 0.7 all-gather.3.cloned.1.call-update
  7.3 3.0 %collective-permute-start = (bf16[128,1024]{1,0:T(8,128)(2,1)}, bf16[128,1024]{1,0:T(8,128)(2,1)S(1)}, u32[]{:S(2)}, u32[]{:S(2)}) collective-permute-start(bf16[128,1024]{1,0:T(8,128)(2,1)} %param.10), channel_id=1, source_target_pairs={{0,2},{2,0},{4,6},{6,4},{8,10},{10,8},{12,14},{14,12},{1,3},{3,1},... | collective-permute-start | bytes 786440 | tf_op jit(solution)/shard_map/ppermute | solution.py:16
  11.0 1.3 gather_fusion
  12.5 1.3 gather_fusion.1
  14.8 2.0 collective-permute-done
  16.8 2.0 maximum_select_fusion.3
  18.8 1.8 collective-permute-start.1
  21.3 2.4 gather_fusion.2
  23.6 2.4 multiply_reduce_fusion
  26.0 14.7 %collective-permute-done.1 = bf16[256,1024]{1,0:T(8,128)(2,1)} collective-permute-done((bf16[256,1024]{1,0:T(8,128)(2,1)}, bf16[256,1024]{1,0:T(8,128)(2,1)}, u32[]{:S(2)}, u32[]{:S(2)}) %collective-permute-start.1) | collective-permute-done | bytes 524320 | tf_op jit(solution)/shard_map/ppermute | solution.py:16
  40.7 3.0 %maximum_select_fusion.2 = bf16[512,1024]{1,0:T(8,128)(2,1)} fusion(bf16[256,1024]{1,0:T(8,128)(2,1)} %collective-permute-done.1, bf16[256,1024]{1,0:T(8,128)(2,1)} %maximum_select_fusion.3, pred[]{:T(512)S(6)} %eq.55), kind=kLoop, calls=%fused_computation.50 | loop fusion | flops 4718592 | bytes 2097153 | tf_op jit(solution)/shard_map/jit(_where)/select_n | solution.py:19
  43.7 2.5 collective-permute-start.2
  46.9 82.5 %all-gather = bf16[8,2,1024]{2,1,0:T(2,128)(2,1)S(1)} all-gather(bf16[1,2,1024]{2,1,0:T(2,128)(2,1)S(1)} %bitcast.193), channel_id=1, replica_groups=mesh['groups'=2,'passage'=8,'tensor'=2] {'passage'}, dimensions={0}, use_global_device_ids=true | all-gather | bytes 36864 | tf_op jit(solution)/shard_map/all_gather | solution.py:77
  131.4 0.7 iota_compare_fusion.3
  132.7 2.2 fusion
  135.0 6.2 %convolution_convert_fusion = bf16[1280,1024]{0,1:T(8,128)(2,1)S(1)} fusion(bf16[1280,1024]{1,0:T(8,128)(2,1)S(1)} %fusion, bf16[512,1024]{1,0:T(8,128)(2,1)} %collective-permute-done.2, bf16[512,1024]{1,0:T(8,128)(2,1)} %maximum_select_fusion.2, pred[]{:T(512)S(6)} %eq.54), kind=kOutput, calls=%fused_computation.6 | convolution fusion | flops 2695102464 | bytes 7340033 | tf_op jit(solution)/shard_map/dot_general | solution.py:72
  141.3 1.5 fusion.104
  142.8 5.3 %convolution_convert_fusion.1 = bf16[1280,1024]{0,1:T(8,128)(2,1)S(1)} fusion(bf16[1280,1024]{1,0:T(8,128)(2,1)} %copy-done.1, bf16[1024,1024]{1,0:T(8,128)(2,1)} %all-gather.3.cloned.1.call-done), kind=kOutput, calls=%fused_computation.7 | convolution fusion | flops 2685665280 | bytes 7340032 | tf_op jit(solution)/shard_map/dot_general | solution.py:71
  148.3 0.9 fusion.111
  149.2 0.9 fusion.107
  150.4 0.9 fusion.110
  151.6 0.7 copy-done.2
  152.5 17.8 %pmax.7 = f32[16,16]{0,1:T(8,128)S(1)} all-reduce(f32[16,16]{0,1:T(8,128)S(1)} %get-tuple-element.17), channel_id=1, replica_groups=mesh['groups'=2,'passage'=8,'tensor'=2] {'passage'}, use_global_device_ids=true, to_apply=%region_9.10 | all-reduce | flops 256 | bytes 2048 | tf_op jit(solution)/shard_map/pmax | solution.py:113
  170.3 1.4 fusion.32
  171.7 1.3 fusion.36
  173.1 1.4 fusion.31
  174.5 1.4 fusion.28
  176.3 0.9 fusion.22
  177.6 0.7 reshape.298
  178.4 19.1 %all-reduce.1 = f32[16,16]{0,1:T(8,128)S(1)} all-reduce(f32[16,16]{0,1:T(8,128)S(1)} %get-tuple-element.34), channel_id=3, replica_groups=mesh['groups'=2,'passage'=8,'tensor'=2] {'passage'}, use_global_device_ids=true, to_apply=%region_16.17.clone | all-reduce | flops 256 | bytes 2048
  197.8 47.7 %all-reduce.4.cloned.1.call-done = f32[16,1024]{1,0:T(8,128)} async-done(((f32[16,1024]{1,0:T(8,128)}), f32[16,1024]{1,0:T(8,128)}) %all-reduce.4.cloned.1.call-update) | async-done | bytes 65552
  245.4 1.4 fusion.87
  (72 shorter events, 7.0 us)
Async XLA Ops:
  6.5 14.7 %copy-start = (bf16[6,256,1024]{2,1,0:T(8,128)(2,1)S(1)}, bf16[6,256,1024]{2,1,0:T(8,128)(2,1)}, u32[]{:S(2)}) copy-start(bf16[6,256,1024]{2,1,0:T(8,128)(2,1)} %param.7) | copy-start | bytes 9437188
  6.5 136.3 %all-gather.3.cloned.1.call-start = ((), (), s32[]{:S(2)}) async-start(), calls=%async_computation | async-start | bytes 2359296 | tf_op jit(solution)/shard_map/all_gather | solution.py:66
  7.3 238.2 %all-reduce.4.cloned.1.call-start = ((), (), s32[]{:S(2)}) async-start(), calls=%async_computation.1 | async-start | bytes 131072
  7.3 9.5 %collective-permute-start = (bf16[128,1024]{1,0:T(8,128)(2,1)}, bf16[128,1024]{1,0:T(8,128)(2,1)S(1)}, u32[]{:S(2)}, u32[]{:S(2)}) collective-permute-start(bf16[128,1024]{1,0:T(8,128)(2,1)} %param.10), channel_id=1, source_target_pairs={{0,2},{2,0},{4,6},{6,4},{8,10},{10,8},{12,14},{14,12},{1,3},{3,1},... | collective-permute-start | bytes 786440 | tf_op jit(solution)/shard_map/ppermute | solution.py:16
  18.8 21.9 %collective-permute-start.1 = (bf16[256,1024]{1,0:T(8,128)(2,1)}, bf16[256,1024]{1,0:T(8,128)(2,1)}, u32[]{:S(2)}, u32[]{:S(2)}) collective-permute-start(bf16[256,1024]{1,0:T(8,128)(2,1)} %maximum_select_fusion.3), channel_id=1, source_target_pairs={{0,4},{2,6},{4,0},{6,2},{8,12},{10,14},{12,8},{14,10},{1,5},{3,7},... | collective-permute-start | bytes 1572872 | tf_op jit(solution)/shard_map/ppermute | solution.py:16
  21.2 149.1 %copy-start.10 = (pred[256]{0:T(512)(128)(4,1)}, pred[256]{0:T(512)(128)(4,1)S(1)}, u32[]{:S(2)}) copy-start(pred[256]{0:T(512)(128)(4,1)S(1)} %iota_compare_fusion.4) | copy-start | bytes 772
  23.6 23.3 %copy-start.14 = (bf16[2,1024]{1,0:T(2,128)(2,1)S(1)}, bf16[2,1024]{1,0:T(2,128)(2,1)}, u32[]{:S(2)}) copy-start(bf16[2,1024]{1,0:T(2,128)(2,1)} %param.8) | copy-start | bytes 12292
  23.6 105.9 %copy-start.16 = (u32[32]{0:T(128)S(1)}, u32[32]{0:T(128)}, u32[]{:S(2)}) copy-start(u32[32]{0:T(128)} %constant.73) | copy-start | bytes 388
  43.7 91.3 %collective-permute-start.2 = (bf16[512,1024]{1,0:T(8,128)(2,1)}, bf16[512,1024]{1,0:T(8,128)(2,1)}, u32[]{:S(2)}, u32[]{:S(2)}) collective-permute-start(bf16[512,1024]{1,0:T(8,128)(2,1)} %maximum_select_fusion.2), channel_id=1, source_target_pairs={{0,8},{2,10},{4,12},{6,14},{8,0},{10,2},{12,4},{14,6},{1,9},{3,11}... | collective-permute-start | bytes 3145736 | tf_op jit(solution)/shard_map/ppermute | solution.py:16
  46.9 102.3 %copy-start.15 = (pred[256]{0:T(512)(128)(4,1)}, pred[256]{0:T(512)(128)(4,1)S(1)}, u32[]{:S(2)}) copy-start(pred[256]{0:T(512)(128)(4,1)S(1)} %iota_compare_fusion.5) | copy-start | bytes 772
  131.4 18.7 %copy-start.11 = (pred[256]{0:T(512)(128)(4,1)}, pred[256]{0:T(512)(128)(4,1)S(1)}, u32[]{:S(2)}) copy-start(pred[256]{0:T(512)(128)(4,1)S(1)} %iota_compare_fusion.2) | copy-start | bytes 772
  132.1 18.3 %copy-start.12 = (pred[256]{0:T(512)(128)(4,1)}, pred[256]{0:T(512)(128)(4,1)S(1)}, u32[]{:S(2)}) copy-start(pred[256]{0:T(512)(128)(4,1)S(1)} %iota_compare_fusion.3) | copy-start | bytes 772
  132.7 18.8 %copy-start.8 = (pred[256]{0:T(512)(128)(4,1)}, pred[256]{0:T(512)(128)(4,1)S(1)}, u32[]{:S(2)}) copy-start(pred[256]{0:T(512)(128)(4,1)S(1)} %iota_compare_fusion.1) | copy-start | bytes 772
  135.0 6.3 %copy-start.1 = (bf16[1280,1024]{1,0:T(8,128)(2,1)}, bf16[1280,1024]{1,0:T(8,128)(2,1)S(1)}, u32[]{:S(2)}) copy-start(bf16[1280,1024]{1,0:T(8,128)(2,1)S(1)} %fusion) | copy-start | bytes 7864324
  151.5 0.7 copy-start.2
  170.3 5.7 %copy-start.4 = (f32[16,16,256]{2,1,0:T(8,128)S(1)}, f32[16,16,256]{2,1,0:T(8,128)}, u32[]{:S(2)}) copy-start(f32[16,16,256]{2,1,0:T(8,128)} %get-tuple-element.57) | copy-start | bytes 786436
  170.3 5.7 %copy-start.7 = (bf16[256,1024]{0,1:T(8,128)(2,1)S(1)}, bf16[256,1024]{0,1:T(8,128)(2,1)}, u32[]{:S(2)}) copy-start(bf16[256,1024]{0,1:T(8,128)(2,1)} %get-tuple-element.24) | copy-start | bytes 1572868
  170.3 5.7 %copy-start.13 = (pred[256]{0:T(512)(128)(4,1)S(1)}, pred[256]{0:T(512)(128)(4,1)}, u32[]{:S(2)}) copy-start(pred[256]{0:T(512)(128)(4,1)} %copy-done.12) | copy-start | bytes 772
  170.3 6.0 %copy-start.6 = (bf16[256,1024]{0,1:T(8,128)(2,1)S(1)}, bf16[256,1024]{0,1:T(8,128)(2,1)}, u32[]{:S(2)}) copy-start(bf16[256,1024]{0,1:T(8,128)(2,1)} %get-tuple-element.23) | copy-start | bytes 1572868
  171.7 5.5 %copy-start.3 = (f32[16,16,256]{2,1,0:T(8,128)S(1)}, f32[16,16,256]{2,1,0:T(8,128)}, u32[]{:S(2)}) copy-start(f32[16,16,256]{2,1,0:T(8,128)} %copy-done.2) | copy-start | bytes 786436
  171.7 5.5 %copy-start.5 = (bf16[256,1024]{0,1:T(8,128)(2,1)S(1)}, bf16[256,1024]{0,1:T(8,128)(2,1)}, u32[]{:S(2)}) copy-start(bf16[256,1024]{0,1:T(8,128)(2,1)} %get-tuple-element.22) | copy-start | bytes 1572868
  171.7 5.5 %copy-start.9 = (pred[256]{0:T(512)(128)(4,1)S(1)}, pred[256]{0:T(512)(128)(4,1)}, u32[]{:S(2)}) copy-start(pred[256]{0:T(512)(128)(4,1)} %copy-done.8) | copy-start | bytes 772
Sparse Core Ops, SparseCore 0:
  9.5 86.3 all-gather.2
  178.5 66.9 all-reduce.3
